TPU v7x, 256 devices: a whole 4x4x8 slice. The times are simulated.
256 devices in a mesh: segment: 16 (over y_lo, x, core), ctx: 16 (over y_hi, z).
Axes of the slice: x: 4, y: 4 (y_hi: 2, y_lo: 2; y = y_hi * 2 + y_lo), z: 8, core: 2. Of those that a mesh axis runs over, the one named last changes fastest.
Arguments:
- carried_down: bfloat16 [16, 2048, 1408], P('segment', 'ctx'), may hold values from -6 to 6
- carried_up: bfloat16 [16, 2048, 1408], P('segment', 'ctx'), may hold values from -6 to 6
- skip_bank: bfloat16 [16, 3, 2048, 1408], P('segment', None, 'ctx'), may hold values from -6 to 6
- queue: bfloat16 [8, 2048, 1408], P(None, 'ctx'), may hold values from -6 to 6
- next_entry: int32 [8], replicated, may hold values from 0 to 7, each once
- skip_slot: int32 [2, 16], P(None, 'segment'), may hold values from 0 to 2
- w_qkv: bfloat16 [16, 3, 1408, 1408], P('segment', None, 'ctx'), may hold values from -1.6523056 to 1.6523056
- w_out: bfloat16 [16, 1408, 1408], P('segment', 'ctx'), may hold values from -0.5 to 0.5
- w_skip: bfloat16 [16, 2816, 1408], P('segment', 'ctx'), may hold values from -0.109375 to 0.109375
- gains: float32 [16, 2, 1408], P('segment'), may hold values from 0.1 to 1.9
Outputs:
- desc_out: bfloat16 [2, 16, 2048, 1408], P(None, 'segment', 'ctx')
- asc_out: bfloat16 [2, 16, 2048, 1408], P(None, 'segment', 'ctx')
All inputs are finite; a program needn't handle non-finite values.
Results may differ from a plain program's by a relative error of at most 0.015.
Values may be sent and summed in bfloat16 or wider, within the bound.
A program may use at most 128 MiB of HBM per device.

v0:
```python
import jax
import jax.numpy as jnp
from jax import lax
from jax.sharding import PartitionSpec as P

HEAD = 88
D = 1408


def from_behind(value, axis, steps):
    count = lax.axis_size(axis)
    leading, last = (max(0, -steps), min(count, count - steps))
    return lax.ppermute(value, axis, [(source, source + steps) for source in range(leading, last)])


def layer_norm(values, gain):
    center = values - jnp.mean(values, axis=-1, keepdims=True)
    spread = jnp.mean(center * center, axis=-1, keepdims=True)
    return center * lax.rsqrt(spread + 1e-06) * gain


def attend(stacked):
    queries, keys, values = (stacked[0], stacked[1], stacked[2])
    local_heads, width, length = queries.shape
    block = 512
    blocks = length // block
    grouped = queries.reshape(local_heads, width, blocks, block).transpose(2, 0, 1, 3)

    def one_block(query_block):
        scores = jnp.einsum(
            "hen,hem->hnm", query_block, keys, preferred_element_type=jnp.float32
        ) * HEAD ** (-0.5)
        peak = jnp.max(scores, axis=2, keepdims=True)
        powers = jnp.exp(scores - peak)
        totals = jnp.sum(powers, axis=2)
        mixed = jnp.einsum(
            "hem,hnm->hen", values, powers.astype(jnp.bfloat16), preferred_element_type=jnp.float32
        )
        return (mixed / totals[:, None, :]).astype(jnp.bfloat16)

    results = lax.map(one_block, grouped)
    return results.transpose(1, 2, 0, 3).reshape(local_heads, width, length)


def send_down(descended):
    return from_behind(descended, "segment", 1)


def send_up(ascended):
    return from_behind(ascended, "segment", -1)


def on_device(
    carried_down, carried_up, skip_bank, queue, next_entry, skip_slot, w_qkv, w_out, w_skip, gains
):
    segment_count = lax.axis_size("segment")
    place = lax.axis_index("segment")
    tok_rows = carried_down.shape[1]
    local_heads = w_qkv.shape[2] // HEAD
    full_out, full_skip = (
        lax.all_gather(w_out[0], "ctx", axis=0, tiled=True),
        lax.all_gather(w_skip[0], "ctx", axis=0, tiled=True),
    )
    own_qkv = w_qkv[0].reshape(3, local_heads, HEAD, D)

    def descend(inputs):
        normed = layer_norm(inputs.astype(jnp.float32), gains[0, 0]).astype(jnp.bfloat16)
        made = jnp.einsum(
            "khed,td->khet",
            own_qkv,
            lax.all_gather(normed, "ctx", axis=0, tiled=True),
            preferred_element_type=jnp.float32,
        )
        projected = made.astype(jnp.bfloat16)
        head_out = attend(projected)
        returned = lax.all_to_all(head_out, "ctx", split_axis=2, concat_axis=0, tiled=True)
        merged = returned.reshape(D, tok_rows)
        added = jnp.einsum("ft,fd->td", merged, full_out, preferred_element_type=jnp.float32)
        return (inputs.astype(jnp.float32) + added).astype(jnp.bfloat16)

    def ascend(rising, slot):
        skip = lax.dynamic_index_in_dim(skip_bank[0], slot, 0, keepdims=False)
        joined = jnp.concatenate([rising, skip], axis=1)
        projected = jnp.dot(joined, full_skip, preferred_element_type=jnp.float32)
        return layer_norm(projected, gains[0, 1]).astype(jnp.bfloat16)

    first_down = descend(carried_down[0])
    first_up = ascend(carried_up[0], skip_slot[0, 0])
    arrive_down = send_down(first_down)
    arrive_up = send_up(first_up)
    entering = lax.dynamic_index_in_dim(queue, next_entry[0], 0, keepdims=False)
    down_next = jnp.where(place == 0, entering, arrive_down)
    up_next = jnp.where(place == segment_count - 1, first_down, arrive_up)
    second_down = descend(down_next)
    second_up = ascend(up_next, skip_slot[1, 0])
    desc_out = jnp.stack([first_down, second_down])[:, None]
    asc_out = jnp.stack([first_up, second_up])[:, None]
    return (desc_out, asc_out)


def solution(mesh):
    in_specs = (
        P("segment", "ctx", None),
        P("segment", "ctx", None),
        P("segment", None, "ctx", None),
        P(None, "ctx", None),
        P(),
        P(None, "segment"),
        P("segment", None, "ctx", None),
        P("segment", "ctx", None),
        P("segment", "ctx", None),
        P("segment", None, None),
    )
    out_specs = (P(None, "segment", "ctx", None), P(None, "segment", "ctx", None))
    return jax.shard_map(
        on_device, mesh=mesh, in_specs=in_specs, out_specs=out_specs, check_vma=False
    )
```

profile of v0, /device:TPU:32, one launch (start us, length us, event | category | flops | bytes accessed | tf_op | source)
XLA Modules:
  0.0 543.4 jit_solution(12254006201471091412)
XLA Ops:
  7.2 0.8 slice_reduce_fusion
  8.0 1.1 convert_reduce_fusion.1
  9.2 1.2 fusion.95
  10.4 2.0 fusion.97
  12.5 0.7 all-gather.13.cloned.1.call-update
  13.2 0.7 all-gather.11.cloned.1.call-update
  13.9 1.3 fusion.109
  18.8 1.9 dynamic-slice_bitcast_fusion.1
  20.7 105.0 %all-gather.7.cloned.1.call-done = bf16[2048,1408]{1,0:T(8,128)(2,1)} async-done(((bf16[128,1408]{1,0:T(8,128)(2,1)}), bf16[2048,1408]{1,0:T(8,128)(2,1)}) %all-gather.7.cloned.1.call-update) | async-done | bytes 5767184 | tf_op jit(solution)/shard_map/all_gather | solution.py:71
  125.7 4.5 fusion.73
  130.3 10.5 %while.20 = (s32[]{:T(128)}, bf16[4,1,88,512]{3,2,1,0:T(8,128)(2,1)S(1)}, bf16[4,1,88,512]{3,2,1,0:T(8,128)(2,1)S(1)}, bf16[1,88,2048]{2,1,0:T(8,128)(2,1)S(1)}, bf16[1,88,2048]{2,1,0:T(8,128)(2,1)S(1)}, /*index=5*/s32[]{:T(128)}) while((s32[]{:T(128)}, bf16[4,1,88,512]{3,2,1,0:T(8,128)(2,1)S(1)}, bf16[4,1,88,512]{3,2,1,0:T(8,128)(2,1)S(1)}, ...), condition=%wide.region_5.6_spmd, body=%wide.region_2.5_spmd.sunk | while | flops 377576448 | bytes 13494349 | solution.py:41
  130.4 0.8 multiply_reduce_fusion.6
  131.2 0.8 fusion.125
  132.0 1.0 fusion.126
  133.0 0.8 multiply_reduce_fusion.6
  133.8 0.8 fusion.125
  134.6 1.0 fusion.126
  135.6 0.8 multiply_reduce_fusion.6
  136.4 0.8 fusion.125
  137.2 1.0 fusion.126
  138.2 0.8 multiply_reduce_fusion.6
  139.0 0.8 fusion.125
  139.9 1.0 fusion.126
  141.9 11.5 %reduce.13 = bf16[2048,88]{1,0:T(8,128)(2,1)S(1)} reduce(bf16[2048,1,88]{2,1,0:T(2,128)(2,1)S(1)} %bitcast.194, bf16[]{:T(256)} %broadcast.140), dimensions={1}, to_apply=%bitcast.149.reduce_sub_computation | reduce | bytes 720898
  153.5 1.9 reshape.170
  155.4 5.2 all-to-all-start
  160.8 100.3 %all-gather.13.cloned.1.call-done = bf16[1,2816,1408]{2,1,0:T(8,128)(2,1)} async-done(((bf16[1,176,1408]{2,1,0:T(8,128)(2,1)}), bf16[1,2816,1408]{2,1,0:T(8,128)(2,1)}) %all-gather.13.cloned.1.call-update) | async-done | bytes 7929872 | tf_op jit(solution)/shard_map/all_gather | solution.py:62
  261.1 4.7 fusion.110
  266.0 0.9 multiply_convert_fusion.1
  266.9 1.3 collective-permute-start.1
  268.2 2.1 reshape.171
  270.3 0.6 copy.35
  271.2 89.2 %all-gather.11.cloned.1.call-done = bf16[1,1408,1408]{2,1,0:T(8,128)(2,1)} async-done(((bf16[1,88,1408]{2,1,0:T(8,128)(2,1)}), bf16[1,1408,1408]{2,1,0:T(8,128)(2,1)}) %all-gather.11.cloned.1.call-update) | async-done | bytes 3964944 | tf_op jit(solution)/shard_map/all_gather | solution.py:61
  360.4 3.1 broadcast_select_fusion
  363.5 1.3 collective-permute-start
  364.9 1.1 collective-permute-done
  366.1 1.2 convert_reduce_fusion
  367.5 1.0 fusion.94
  368.5 0.9 fusion.114
  369.5 4.7 fusion.111
  374.1 0.8 copy-done.2
  375.2 106.9 %all-gather.9.cloned.1.call-done = bf16[2048,1408]{1,0:T(8,128)(2,1)} async-done(((bf16[128,1408]{1,0:T(8,128)(2,1)}), bf16[2048,1408]{1,0:T(8,128)(2,1)}) %all-gather.9.cloned.1.call-update) | async-done | bytes 5767184 | tf_op jit(solution)/shard_map/all_gather | solution.py:71
  482.1 4.5 fusion.70
  486.8 10.7 %while.21 = (s32[]{:T(128)}, bf16[4,1,88,512]{3,2,1,0:T(8,128)(2,1)S(1)}, bf16[4,1,88,512]{3,2,1,0:T(8,128)(2,1)S(1)}, bf16[1,88,2048]{2,1,0:T(8,128)(2,1)S(1)}, bf16[1,88,2048]{2,1,0:T(8,128)(2,1)S(1)}, /*index=5*/s32[]{:T(128)}) while((s32[]{:T(128)}, bf16[4,1,88,512]{3,2,1,0:T(8,128)(2,1)S(1)}, bf16[4,1,88,512]{3,2,1,0:T(8,128)(2,1)S(1)}, ...), condition=%wide.region_11.12_spmd, body=%wide.region_8.11_spmd.sunk | while | flops 377576448 | bytes 13494349 | solution.py:41
  487.0 0.8 multiply_reduce_fusion.7
  487.9 0.8 fusion.129
  488.7 1.0 fusion.130
  489.7 0.8 multiply_reduce_fusion.7
  490.5 0.8 fusion.129
  491.3 1.0 fusion.130
  492.3 0.8 multiply_reduce_fusion.7
  493.1 0.8 fusion.129
  493.9 1.0 fusion.130
  494.9 0.8 multiply_reduce_fusion.7
  495.7 0.8 fusion.129
  496.5 1.0 fusion.130
  498.1 11.5 %reduce.14 = bf16[2048,88]{1,0:T(8,128)(2,1)S(1)} reduce(bf16[2048,1,88]{2,1,0:T(2,128)(2,1)S(1)} %bitcast.195, bf16[]{:T(256)} %broadcast.140), dimensions={1}, to_apply=%bitcast.151.reduce_sub_computation | reduce | bytes 720898
  509.6 1.9 reshape.172
  511.5 5.2 all-to-all-start.1
  516.8 11.6 %all-to-all-done.1 = bf16[16,2,5632]{2,1,0:T(2,128)(2,1)} async-done(((bf16[16,2,5632]{2,1,0:T(2,128)(2,1)}), bf16[16,2,5632]{2,1,0:T(2,128)(2,1)}, u32[]{:S(2)}, u32[]{:S(2)}) %all-to-all-start.1) | async-done | bytes 360480 | tf_op jit(solution)/shard_map/all_to_all | solution.py:76
  528.4 3.4 reshape.173
  531.8 0.6 copy.40
  532.7 2.9 fusion.82
  535.6 1.3 maximum_bitcast_fusion
  (56 shorter events, 3.5 us)
Async XLA Ops:
  7.2 118.5 %copy-start = (bf16[1,3,88,1408]{3,2,1,0:T(8,128)(2,1)S(1)}, bf16[1,3,88,1408]{3,2,1,0:T(8,128)(2,1)}, u32[]{:S(2)}) copy-start(bf16[1,3,88,1408]{3,2,1,0:T(8,128)(2,1)} %param.20) | copy-start | bytes 2230276
  7.2 118.5 %all-gather.7.cloned.1.call-start = ((), (), s32[]{:S(2)}) async-start(), calls=%async_computation.2 | async-start | bytes 6127616 | tf_op jit(solution)/shard_map/all_gather | solution.py:71
  12.4 248.7 %all-gather.13.cloned.1.call-start = ((), (), s32[]{:S(2)}) async-start(), calls=%async_computation.5 | async-start | bytes 8425472 | tf_op jit(solution)/shard_map/all_gather | solution.py:62
  13.2 347.2 %all-gather.11.cloned.1.call-start = ((), (), s32[]{:S(2)}) async-start(), calls=%async_computation.4 | async-start | bytes 4212736 | tf_op jit(solution)/shard_map/all_gather | solution.py:61
  140.8 120.3 %copy-start.9 = (bf16[1,128,1408]{2,1,0:T(8,128)(2,1)S(1)}, bf16[1,128,1408]{2,1,0:T(8,128)(2,1)}, u32[]{:S(2)}) copy-start(bf16[1,128,1408]{2,1,0:T(8,128)(2,1)} %param.15) | copy-start | bytes 1081348
  155.4 112.9 %all-to-all-start = ((bf16[16,2,5632]{2,1,0:T(2,128)(2,1)}), bf16[16,2,5632]{2,1,0:T(2,128)(2,1)S(1)}, u32[]{:S(2)}, u32[]{:S(2)}) async-start(bf16[16,2,5632]{2,1,0:T(2,128)(2,1)} %reshape.170), calls=%async_computation | async-start | bytes 720896 | tf_op jit(solution)/shard_map/all_to_all | solution.py:76
  160.6 321.6 %all-gather.9.cloned.1.call-start = ((), (), s32[]{:S(2)}) async-start(), calls=%async_computation.3 | async-start | bytes 6127616 | tf_op jit(solution)/shard_map/all_gather | solution.py:71
  265.8 94.6 %copy-start.1 = (bf16[1,128,1408]{2,1,0:T(8,128)(2,1)S(1)}, bf16[1,128,1408]{2,1,0:T(8,128)(2,1)}, u32[]{:S(2)}) copy-start(bf16[1,128,1408]{2,1,0:T(8,128)(2,1)} %param.14) | copy-start | bytes 1081348
  266.9 93.4 %collective-permute-start.1 = (bf16[128,1408]{1,0:T(8,128)(2,1)}, bf16[128,1408]{1,0:T(8,128)(2,1)}, u32[]{:S(2)}, u32[]{:S(2)}) collective-permute-start(bf16[128,1408]{1,0:T(8,128)(2,1)} %multiply_convert_fusion.1), channel_id=1, source_target_pairs={{16,0},{32,16},{48,32},{64,48},{80,64},{96,80},{112,96},{128,112},... | collective-permute-start | bytes 1081352 | tf_op jit(solution)/shard_map/ppermute | solution.py:13
  271.0 93.8 %copy-start.8 = (s32[8]{0:T(128)S(1)}, s32[8]{0:T(128)}, u32[]{:S(2)}) copy-start(s32[8]{0:T(128)} %param.18) | copy-start | bytes 100
  360.4 9.1 %copy-start.7 = (bf16[128,1408]{1,0:T(8,128)(2,1)S(1)}, bf16[128,1408]{1,0:T(8,128)(2,1)}, u32[]{:S(2)}) copy-start(bf16[128,1408]{1,0:T(8,128)(2,1)} %get-tuple-element.95) | copy-start | bytes 1081348
  363.5 10.6 %copy-start.5 = (bf16[128,1408]{1,0:T(8,128)(2,1)}, bf16[128,1408]{1,0:T(8,128)(2,1)S(1)}, u32[]{:S(2)}) copy-start(bf16[128,1408]{1,0:T(8,128)(2,1)S(1)} %get-tuple-element.107) | copy-start | bytes 1081348
  363.5 2.6 collective-permute-start
  374.1 0.9 copy-start.2
  497.5 19.1 %copy-start.3 = (f32[128,1408]{1,0:T(8,128)S(1)}, f32[128,1408]{1,0:T(8,128)}, u32[]{:S(2)}) copy-start(f32[128,1408]{1,0:T(8,128)} %copy-done.2) | copy-start | bytes 2162692
  511.5 17.0 %all-to-all-start.1 = ((bf16[16,2,5632]{2,1,0:T(2,128)(2,1)}), bf16[16,2,5632]{2,1,0:T(2,128)(2,1)}, u32[]{:S(2)}, u32[]{:S(2)}) async-start(bf16[16,2,5632]{2,1,0:T(2,128)(2,1)} %reshape.172), calls=%async_computation.1 | async-start | bytes 720896 | tf_op jit(solution)/shard_map/all_to_all | solution.py:76
  531.8 3.8 copy-start.4
  532.4 3.2 copy-start.6
Sparse Core Ops, SparseCore 0:
  12.5 113.0 all-gather.6
  128.3 132.7 all-gather.12
  263.8 96.5 all-gather.10
  368.7 113.4 all-gather.8
where the time goes:
time: 544 us; the launch traced here: 543 us
  waiting for transfers between devices  416 us (76%)
  other arithmetic  40.2 us (7%)
  matrix products  38.6 us (7%)
  between operations  17.9 us (3%)
  local copies, waits for them, and re-layouts  17.5 us (3%)
  starting transfers between devices  13.3 us (2%)
    all_gather x2, waiting for transfers between devices, descend(): lax.all_gather(normed, 'ctx', axis=0, tiled=True)  212 us
    all_gather x1, waiting for transfers between devices, on_device(): lax.all_gather(w_skip[0], 'ctx', axis=0, tiled=True)  100 us
    all_gather x1, waiting for transfers between devices, on_device(): lax.all_gather(w_out[0], 'ctx', axis=0, tiled=True)  89.2 us
    unnamed x3, other arithmetic  24.3 us
    all_to_all x2, waiting for transfers between devices, descend(): lax.all_to_all(head_out, 'ctx', split_axis=2, concat_axis=0, tiled=True)  11.6 us
  transfers between devices with their start and end apart: 8, of which 6 were waited for; matrix products, arithmetic and copies ran while one was open for 9% of the time, Pallas kernels for 0%

commit v1 on v0

--- a/solution.py
+++ b/solution.py
@@ -68,7 +68,9 @@
         made = jnp.einsum(
             "khed,td->khet",
             own_qkv,
-            lax.all_gather(normed, "ctx", axis=0, tiled=True),
+            jnp.concatenate(
+                lax.all_to_all(jnp.stack([normed] * lax.axis_size("ctx")), "ctx", 0, 0), axis=0
+            ),
             preferred_element_type=jnp.float32,
         )
         projected = made.astype(jnp.bfloat16)

time: 544 us -> 564 us (1.037); the launches traced: 543 us -> 557 us
  starting transfers between devices: 13.3 us -> 43.8 us
  waiting for transfers between devices: 416 us -> 396 us
    all_to_all x0 -> x2, waiting for transfers between devices: none -> 270 us  [descend(): lax.all_to_all(jnp.stack([normed] * lax.axis_size('ctx')), 'ctx', 0, 0)]
    all_gather x2 -> x0, waiting for transfers between devices: 212 us -> none  [descend(): lax.all_gather(normed, 'ctx', axis=0, tiled=True)]
    all_gather x1, waiting for transfers between devices: 100 us -> 22.9 us  [on_device(): lax.all_gather(w_skip[0], 'ctx', axis=0, tiled=True)]
    all_to_all x0 -> x2, starting transfers between devices: none -> 16.6 us  [descend(): lax.all_to_all(jnp.stack([normed] * lax.axis_size('ctx')), 'ctx', 0, 0)]
    all_to_all x2, starting transfers between devices: 10.4 us -> 24.5 us  [descend(): lax.all_to_all(head_out, 'ctx', split_axis=2, concat_axis=0, tiled=True)]
    another operation x2 -> x4, local copies, waits for them, and re-layouts: 0.05 us -> 6.15 us  [the longest x2 6.1 us: descend(): jnp.stack([normed] * lax.axis_size('ctx'))]
  transfers between devices with their start and end apart: 8 -> 8, of which waited for: 6 -> 6; matrix products, arithmetic and copies ran while one was open for 9% -> 10% of each run, Pallas kernels for 0% -> 0%
where the time goes in v1:
time: 564 us; the launch traced here: 557 us
  waiting for transfers between devices  396 us (70%)
  starting transfers between devices  43.8 us (8%)
  other arithmetic  38.7 us (7%)
  matrix products  38.5 us (7%)
  local copies, waits for them, and re-layouts  21.9 us (4%)
  between operations  18.4 us (3%)
    all_to_all x2, waiting for transfers between devices, descend(): lax.all_to_all(jnp.stack([normed] * lax.axis_size('ctx')), 'ctx', 0, 0)  270 us
    all_gather x1, waiting for transfers between devices, on_device(): lax.all_gather(w_out[0], 'ctx', axis=0, tiled=True)  87 us
    all_to_all x2, starting transfers between devices, descend(): lax.all_to_all(head_out, 'ctx', split_axis=2, concat_axis=0, tiled=True)  24.5 us
    unnamed x3, other arithmetic  24.3 us
    all_gather x1, waiting for transfers between devices, on_device(): lax.all_gather(w_skip[0], 'ctx', axis=0, tiled=True)  22.9 us
    all_to_all x2, starting transfers between devices, descend(): lax.all_to_all(jnp.stack([normed] * lax.axis_size('ctx')), 'ctx', 0, 0)  16.6 us
    all_to_all x2, waiting for transfers between devices, descend(): lax.all_to_all(head_out, 'ctx', split_axis=2, concat_axis=0, tiled=True)  13.9 us
  transfers between devices with their start and end apart: 8, of which 6 were waited for; matrix products, arithmetic and copies ran while one was open for 10% of the time, Pallas kernels for 0%

profile of v1, /device:TPU:32, one launch (start us, length us, event | category | flops | bytes accessed | tf_op | source)
XLA Modules:
  0.0 557.3 jit_solution(10299314911701261868)
XLA Ops:
  7.2 0.7 all-gather.7.cloned.1.call-update
  7.9 0.8 slice_reduce_fusion
  8.7 1.1 convert_reduce_fusion.1
  9.9 1.2 fusion.80
  11.1 1.2 fusion.91
  12.3 3.0 stack.19
  15.4 11.3 %all-to-all-start = ((bf16[16,128,1408]{2,1,0:T(8,128)(2,1)}), bf16[16,128,1408]{2,1,0:T(8,128)(2,1)}, u32[]{:S(2)}, u32[]{:S(2)}) async-start(bf16[16,128,1408]{2,1,0:T(8,128)(2,1)} %stack.19), calls=%async_computation | async-start | bytes 11534336 | tf_op jit(solution)/shard_map/all_to_all | solution.py:72
  26.8 0.7 all-gather.5.cloned.1.call-update
  32.0 0.8 dynamic-slice_bitcast_fusion.1
  32.8 148.1 %all-to-all-done = bf16[16,128,1408]{2,1,0:T(8,128)(2,1)} async-done(((bf16[16,128,1408]{2,1,0:T(8,128)(2,1)}), bf16[16,128,1408]{2,1,0:T(8,128)(2,1)}, u32[]{:S(2)}, u32[]{:S(2)}) %all-to-all-start) | async-done | bytes 5767200 | tf_op jit(solution)/shard_map/all_to_all | solution.py:72
  180.9 4.5 fusion.60
  185.6 10.5 %while.20 = (s32[]{:T(128)}, bf16[4,1,88,512]{3,2,1,0:T(8,128)(2,1)S(1)}, bf16[4,1,88,512]{3,2,1,0:T(8,128)(2,1)S(1)}, bf16[1,88,2048]{2,1,0:T(8,128)(2,1)S(1)}, bf16[1,88,2048]{2,1,0:T(8,128)(2,1)S(1)}, /*index=5*/s32[]{:T(128)}) while((s32[]{:T(128)}, bf16[4,1,88,512]{3,2,1,0:T(8,128)(2,1)S(1)}, bf16[4,1,88,512]{3,2,1,0:T(8,128)(2,1)S(1)}, ...), condition=%wide.region_5.6_spmd, body=%wide.region_2.5_spmd.sunk | while | flops 377576448 | bytes 13494349 | solution.py:41
  185.6 0.8 multiply_reduce_fusion.6
  186.4 0.8 fusion.114
  187.2 1.0 fusion.115
  188.2 0.8 multiply_reduce_fusion.6
  189.1 0.8 fusion.114
  189.9 1.0 fusion.115
  190.8 0.8 multiply_reduce_fusion.6
  191.7 0.8 fusion.114
  192.5 1.0 fusion.115
  193.5 0.8 multiply_reduce_fusion.6
  194.3 0.8 fusion.114
  195.1 1.0 fusion.115
  197.2 11.5 %reduce.13 = bf16[2048,88]{1,0:T(8,128)(2,1)S(1)} reduce(bf16[2048,1,88]{2,1,0:T(2,128)(2,1)S(1)} %bitcast.184, bf16[]{:T(256)} %broadcast.153), dimensions={1}, to_apply=%bitcast.137.reduce_sub_computation | reduce | bytes 720898
  208.7 1.9 reshape.201
  210.6 13.5 %all-to-all-start.1 = ((bf16[16,2,5632]{2,1,0:T(2,128)(2,1)}), bf16[16,2,5632]{2,1,0:T(2,128)(2,1)S(1)}, u32[]{:S(2)}, u32[]{:S(2)}) async-start(bf16[16,2,5632]{2,1,0:T(2,128)(2,1)} %reshape.201), calls=%async_computation.1 | async-start | bytes 720896 | tf_op jit(solution)/shard_map/all_to_all | solution.py:78
  224.1 22.9 %all-gather.7.cloned.1.call-done = bf16[1,2816,1408]{2,1,0:T(8,128)(2,1)} async-done(((bf16[1,176,1408]{2,1,0:T(8,128)(2,1)}), bf16[1,2816,1408]{2,1,0:T(8,128)(2,1)}) %all-gather.7.cloned.1.call-update) | async-done | bytes 7929872 | tf_op jit(solution)/shard_map/all_gather | solution.py:62
  247.1 4.7 fusion.97
  252.0 0.9 multiply_convert_fusion.1
  252.9 1.3 collective-permute-start.1
  254.2 2.1 reshape.202
  257.1 87.0 %all-gather.5.cloned.1.call-done = bf16[1,1408,1408]{2,1,0:T(8,128)(2,1)} async-done(((bf16[1,88,1408]{2,1,0:T(8,128)(2,1)}), bf16[1,1408,1408]{2,1,0:T(8,128)(2,1)}) %all-gather.5.cloned.1.call-update) | async-done | bytes 3964944 | tf_op jit(solution)/shard_map/all_gather | solution.py:61
  344.1 3.0 broadcast_select_fusion
  347.2 1.3 collective-permute-start
  348.6 1.1 collective-permute-done
  349.8 1.2 convert_reduce_fusion
  351.5 3.0 stack.21
  354.5 5.2 all-to-all-start.2
  359.8 0.9 fusion.103
  360.7 4.7 fusion.98
  365.4 0.8 copy-done.2
  366.4 121.4 %all-to-all-done.2 = bf16[16,128,1408]{2,1,0:T(8,128)(2,1)} async-done(((bf16[16,128,1408]{2,1,0:T(8,128)(2,1)}), bf16[16,128,1408]{2,1,0:T(8,128)(2,1)}, u32[]{:S(2)}, u32[]{:S(2)}) %all-to-all-start.2) | async-done | bytes 5767200 | tf_op jit(solution)/shard_map/all_to_all | solution.py:72
  487.8 4.5 fusion.61
  492.5 10.5 %while.21 = (s32[]{:T(128)}, bf16[4,1,88,512]{3,2,1,0:T(8,128)(2,1)S(1)}, bf16[4,1,88,512]{3,2,1,0:T(8,128)(2,1)S(1)}, bf16[1,88,2048]{2,1,0:T(8,128)(2,1)S(1)}, bf16[1,88,2048]{2,1,0:T(8,128)(2,1)S(1)}, /*index=5*/s32[]{:T(128)}) while((s32[]{:T(128)}, bf16[4,1,88,512]{3,2,1,0:T(8,128)(2,1)S(1)}, bf16[4,1,88,512]{3,2,1,0:T(8,128)(2,1)S(1)}, ...), condition=%wide.region_11.12_spmd, body=%wide.region_8.11_spmd.sunk | while | flops 377576448 | bytes 13494349 | solution.py:41
  492.5 0.8 multiply_reduce_fusion.7
  493.3 0.8 fusion.118
  494.1 0.9 fusion.119
  495.1 0.8 multiply_reduce_fusion.7
  495.9 0.8 fusion.118
  496.8 1.0 fusion.119
  497.7 0.8 multiply_reduce_fusion.7
  498.6 0.8 fusion.118
  499.4 1.0 fusion.119
  500.3 0.8 multiply_reduce_fusion.7
  501.2 0.8 fusion.118
  502.0 1.0 fusion.119
  503.5 11.5 %reduce.14 = bf16[2048,88]{1,0:T(8,128)(2,1)S(1)} reduce(bf16[2048,1,88]{2,1,0:T(2,128)(2,1)S(1)} %bitcast.185, bf16[]{:T(256)} %broadcast.153), dimensions={1}, to_apply=%bitcast.139.reduce_sub_computation | reduce | bytes 720898
  515.1 1.9 reshape.203
  516.9 11.0 %all-to-all-start.3 = ((bf16[16,2,5632]{2,1,0:T(2,128)(2,1)}), bf16[16,2,5632]{2,1,0:T(2,128)(2,1)}, u32[]{:S(2)}, u32[]{:S(2)}) async-start(bf16[16,2,5632]{2,1,0:T(2,128)(2,1)} %reshape.203), calls=%async_computation.3 | async-start | bytes 720896 | tf_op jit(solution)/shard_map/all_to_all | solution.py:78
  528.1 13.9 %all-to-all-done.3 = bf16[16,2,5632]{2,1,0:T(2,128)(2,1)} async-done(((bf16[16,2,5632]{2,1,0:T(2,128)(2,1)}), bf16[16,2,5632]{2,1,0:T(2,128)(2,1)}, u32[]{:S(2)}, u32[]{:S(2)}) %all-to-all-start.3) | async-done | bytes 360480 | tf_op jit(solution)/shard_map/all_to_all | solution.py:78
  542.0 3.4 reshape.204
  546.3 2.9 fusion.68
  549.2 1.3 maximum_bitcast_fusion
  (60 shorter events, 5.4 us)
Async XLA Ops:
  7.2 173.8 %copy-start = (bf16[1,3,88,1408]{3,2,1,0:T(8,128)(2,1)S(1)}, bf16[1,3,88,1408]{3,2,1,0:T(8,128)(2,1)}, u32[]{:S(2)}) copy-start(bf16[1,3,88,1408]{3,2,1,0:T(8,128)(2,1)} %param.20) | copy-start | bytes 2230276
  7.2 239.9 %all-gather.7.cloned.1.call-start = ((), (), s32[]{:S(2)}) async-start(), calls=%async_computation.5 | async-start | bytes 8425472 | tf_op jit(solution)/shard_map/all_gather | solution.py:62
  15.4 12.1 %copy-start.9 = (s32[2,1]{0,1:T(1,128)S(1)}, s32[2,1]{0,1:T(1,128)}, u32[]{:S(2)}) copy-start(s32[2,1]{0,1:T(1,128)} %param.19) | copy-start | bytes 28
  15.4 16.6 %copy-start.7 = (bf16[1,3,128,1408]{3,2,1,0:T(8,128)(2,1)S(1)}, bf16[1,3,128,1408]{3,2,1,0:T(8,128)(2,1)}, u32[]{:S(2)}) copy-start(bf16[1,3,128,1408]{3,2,1,0:T(8,128)(2,1)} %param.16) | copy-start | bytes 3244036
  15.4 165.5 %all-to-all-start = ((bf16[16,128,1408]{2,1,0:T(8,128)(2,1)}), bf16[16,128,1408]{2,1,0:T(8,128)(2,1)}, u32[]{:S(2)}, u32[]{:S(2)}) async-start(bf16[16,128,1408]{2,1,0:T(8,128)(2,1)} %stack.19), calls=%async_computation | async-start | bytes 11534336 | tf_op jit(solution)/shard_map/all_to_all | solution.py:72
  26.8 317.4 %all-gather.5.cloned.1.call-start = ((), (), s32[]{:S(2)}) async-start(), calls=%async_computation.4 | async-start | bytes 4212736 | tf_op jit(solution)/shard_map/all_gather | solution.py:61
  196.1 51.0 %copy-start.11 = (bf16[1,128,1408]{2,1,0:T(8,128)(2,1)S(1)}, bf16[1,128,1408]{2,1,0:T(8,128)(2,1)}, u32[]{:S(2)}) copy-start(bf16[1,128,1408]{2,1,0:T(8,128)(2,1)} %param.15) | copy-start | bytes 1081348
  210.6 43.6 %all-to-all-start.1 = ((bf16[16,2,5632]{2,1,0:T(2,128)(2,1)}), bf16[16,2,5632]{2,1,0:T(2,128)(2,1)S(1)}, u32[]{:S(2)}, u32[]{:S(2)}) async-start(bf16[16,2,5632]{2,1,0:T(2,128)(2,1)} %reshape.201), calls=%async_computation.1 | async-start | bytes 720896 | tf_op jit(solution)/shard_map/all_to_all | solution.py:78
  251.7 92.4 %copy-start.1 = (bf16[1,128,1408]{2,1,0:T(8,128)(2,1)S(1)}, bf16[1,128,1408]{2,1,0:T(8,128)(2,1)}, u32[]{:S(2)}) copy-start(bf16[1,128,1408]{2,1,0:T(8,128)(2,1)} %param.14) | copy-start | bytes 1081348
  252.9 91.2 %collective-permute-start.1 = (bf16[128,1408]{1,0:T(8,128)(2,1)}, bf16[128,1408]{1,0:T(8,128)(2,1)}, u32[]{:S(2)}, u32[]{:S(2)}) collective-permute-start(bf16[128,1408]{1,0:T(8,128)(2,1)} %multiply_convert_fusion.1), channel_id=1, source_target_pairs={{16,0},{32,16},{48,32},{64,48},{80,64},{96,80},{112,96},{128,112},... | collective-permute-start | bytes 1081352 | tf_op jit(solution)/shard_map/ppermute | solution.py:13
  256.9 91.6 %copy-start.10 = (s32[8]{0:T(128)S(1)}, s32[8]{0:T(128)}, u32[]{:S(2)}) copy-start(s32[8]{0:T(128)} %param.18) | copy-start | bytes 100
  347.2 7.4 %copy-start.5 = (bf16[128,1408]{1,0:T(8,128)(2,1)}, bf16[128,1408]{1,0:T(8,128)(2,1)S(1)}, u32[]{:S(2)}) copy-start(bf16[128,1408]{1,0:T(8,128)(2,1)S(1)} %get-tuple-element.107) | copy-start | bytes 1081348
  347.2 2.6 collective-permute-start
  354.5 6.1 %copy-start.8 = (bf16[128,1408]{1,0:T(8,128)(2,1)S(1)}, bf16[128,1408]{1,0:T(8,128)(2,1)}, u32[]{:S(2)}) copy-start(bf16[128,1408]{1,0:T(8,128)(2,1)} %get-tuple-element.95) | copy-start | bytes 1081348
  354.5 133.3 %all-to-all-start.2 = ((bf16[16,128,1408]{2,1,0:T(8,128)(2,1)}), bf16[16,128,1408]{2,1,0:T(8,128)(2,1)}, u32[]{:S(2)}, u32[]{:S(2)}) async-start(bf16[16,128,1408]{2,1,0:T(8,128)(2,1)} %stack.21), calls=%async_computation.2 | async-start | bytes 11534336 | tf_op jit(solution)/shard_map/all_to_all | solution.py:72
  365.3 0.9 copy-start.2
  503.0 25.0 %copy-start.3 = (f32[128,1408]{1,0:T(8,128)S(1)}, f32[128,1408]{1,0:T(8,128)}, u32[]{:S(2)}) copy-start(f32[128,1408]{1,0:T(8,128)} %copy-done.2) | copy-start | bytes 2162692
  516.9 25.1 %all-to-all-start.3 = ((bf16[16,2,5632]{2,1,0:T(2,128)(2,1)}), bf16[16,2,5632]{2,1,0:T(2,128)(2,1)}, u32[]{:S(2)}, u32[]{:S(2)}) async-start(bf16[16,2,5632]{2,1,0:T(2,128)(2,1)} %reshape.203), calls=%async_computation.3 | async-start | bytes 720896 | tf_op jit(solution)/shard_map/all_to_all | solution.py:78
  545.4 3.8 copy-start.4
  546.1 3.2 copy-start.6
Sparse Core Ops, SparseCore 0:
  10.6 236.4 all-gather.6
  249.7 94.3 all-gather.4
